TPU v7x, 32 devices: a whole 2x2x4 slice. The times are simulated.
32 devices in a mesh: dp: 8 (over z, y), tp: 4 (over x, core).
Axes of the slice: x: 2, y: 2, z: 4, core: 2. Of those that a mesh axis runs over, the one named last changes fastest.
Arguments:
- tokens: bfloat16 [32, 1024, 768], P(('dp', 'tp')), may hold values from -11 to 11
- clip_lengths: int32 [32, 4], P(('dp', 'tp')), may hold values from 1 to 384, as said below
- out_grad: bfloat16 [32, 1024, 768], P(('dp', 'tp')), may hold values from -6 to 6
- w_query: bfloat16 [768, 768], P(('dp', 'tp')), may hold values from -0.21875 to 0.21875
- w_key: bfloat16 [768, 768], P(('dp', 'tp')), may hold values from -0.21875 to 0.21875
- w_value: bfloat16 [768, 768], P(('dp', 'tp')), may hold values from -0.21875 to 0.21875
- w_output: bfloat16 [768, 768], P(('dp', 'tp')), may hold values from -2.5 to 2.5
- gain_attention: bfloat16 [768], P(('dp', 'tp')), may hold values from 0.099609375 to 1.8984375
- gain_feed: bfloat16 [768], P(('dp', 'tp')), may hold values from 0.099609375 to 1.8984375
- w_expand: bfloat16 [768, 3072], P('dp', 'tp'), may hold values from -0.21875 to 0.21875
- w_reduce: bfloat16 [3072, 768], P('tp', 'dp'), may hold values from -0.4375 to 0.4375
Outputs:
- block_out: bfloat16 [32, 1024, 768], P(('dp', 'tp'))
- grad_tokens: float32 [32, 1024, 768], P(('dp', 'tp'))
- grad_w_query: float32 [768, 768], P(('dp', 'tp'))
- grad_w_key: float32 [768, 768], P(('dp', 'tp'))
- grad_w_value: float32 [768, 768], P(('dp', 'tp'))
- grad_w_output: float32 [768, 768], P(('dp', 'tp'))
- grad_gain_attention: float32 [768], P(('dp', 'tp'))
- grad_gain_feed: float32 [768], P(('dp', 'tp'))
- grad_w_expand: float32 [768, 3072], P('dp', 'tp')
- grad_w_reduce: float32 [3072, 768], P('tp', 'dp')
- root_mean_squares: float32 [3], replicated
Inputs may be any that keep to these rules, and one draw needn't show every extreme that they name: Each row of clip_lengths gives the lengths of its 3 clips in order, each at most 384 with one of exactly 384 in every row, then the number of padding slots at the row's end, 1 to 256; a row's entries sum to 1024.
All inputs are finite; a program needn't handle non-finite values.
Results may differ from a plain program's by a relative error of at most 0.015.
Values may be sent and summed in bfloat16 or wider, within the bound.
A program may use at most 192 MiB of HBM per device.

v0:
```python
from functools import partial
import jax
import jax.numpy as jnp
from jax import lax
from jax.sharding import PartitionSpec as P

HEADS = 12
HEAD_DIM = 64
SLOTS = 4


def segment_numbers(lengths, pack_len):
    clip_ends = jnp.cumsum(lengths[:, :-1], axis=-1, dtype=jnp.int32)
    position = jnp.arange(pack_len, dtype=jnp.int32)
    return jnp.sum(
        (position[None, :, None] >= clip_ends[:, None, :]).astype(jnp.int32),
        axis=-1,
        dtype=jnp.int32,
    )


def normalize(array_in):
    average = jnp.mean(array_in, axis=-1, keepdims=True)
    centred = array_in - average
    spread = jnp.mean(centred * centred, axis=-1, keepdims=True)
    inv_scale = lax.rsqrt(spread + 1e-06)
    return (centred * inv_scale, inv_scale)


def norm_back(grad_normed, unit_value, inv_scale, gain_vec):
    scaled = grad_normed * gain_vec
    inner_sum = (
        scaled
        - jnp.mean(scaled, axis=-1, keepdims=True)
        - unit_value * jnp.mean(scaled * unit_value, axis=-1, keepdims=True)
    )
    return (inv_scale * inner_sum, jnp.sum(grad_normed * unit_value, axis=0))


def dot_plain(left_side, right_side):
    return jnp.dot(left_side, right_side, preferred_element_type=jnp.float32)


def dot_first(left_side, right_side):
    return lax.dot_general(
        left_side, right_side, (((0,), (0,)), ((), ())), preferred_element_type=jnp.float32
    )


def dot_last(left_side, right_side):
    return lax.dot_general(
        left_side, right_side, (((1,), (1,)), ((), ())), preferred_element_type=jnp.float32
    )


def split_heads(array_in, rows_dev, pack_len):
    return (
        array_in.reshape(rows_dev, pack_len, HEADS, HEAD_DIM)
        .transpose(0, 2, 1, 3)
        .reshape(rows_dev * HEADS, pack_len, HEAD_DIM)
    )


def merge_heads(array_in, rows_dev, pack_len):
    return (
        array_in.reshape(rows_dev, HEADS, pack_len, HEAD_DIM)
        .transpose(0, 2, 1, 3)
        .reshape(rows_dev * pack_len, HEADS * HEAD_DIM)
    )


def head_scores(query_head, key_head, segments):
    same_clip = segments[:, None] == segments[None, :]
    scores = dot_last(query_head, key_head) * 0.125
    return jnp.where(same_clip, scores, -1e30)


def head_forward(block_item):
    query_head, key_head, value_head, segments = block_item
    scores = head_scores(query_head, key_head, segments)
    row_max = jnp.max(scores, axis=-1, keepdims=True)
    exponent = jnp.exp(scores - row_max)
    row_sum = jnp.sum(exponent, axis=-1, keepdims=True)
    weights = (exponent / row_sum).astype(jnp.bfloat16)
    return (dot_plain(weights, value_head).astype(jnp.bfloat16), row_max, row_sum)


def head_backward(block_item):
    query_head, key_head, value_head, segments, row_max, row_sum, grad_head = block_item
    scores = head_scores(query_head, key_head, segments)
    probabilities = jnp.exp(scores - row_max) / row_sum
    grad_probs = dot_last(grad_head, value_head)
    grad_value = dot_first(probabilities.astype(jnp.bfloat16), grad_head)
    inner_sum = jnp.sum(probabilities * grad_probs, axis=-1, keepdims=True)
    grad_scores = (probabilities * (grad_probs - inner_sum)).astype(jnp.bfloat16)
    grad_query = (dot_plain(grad_scores, key_head) * 0.125).astype(jnp.bfloat16)
    grad_key = (dot_first(grad_scores, query_head) * 0.125).astype(jnp.bfloat16)
    return (grad_query, grad_key, grad_value.astype(jnp.bfloat16))


def on_device(
    tokens,
    clip_lengths,
    out_grad,
    w_query,
    w_key,
    w_value,
    w_output,
    gain_attention,
    gain_feed,
    w_expand,
    w_reduce,
):
    rows_dev, pack_len, width = tokens.shape
    token_count = rows_dev * pack_len
    segments = segment_numbers(clip_lengths, pack_len)
    valid_rows = (segments < SLOTS - 1).astype(jnp.float32).reshape(-1)
    valid_column = valid_rows[:, None]
    inputs = tokens.reshape(token_count, width).astype(jnp.float32)
    query_full, key_full, value_full, output_full, gain_one, gain_two = (
        lax.all_gather(w_query, ("dp", "tp"), axis=0, tiled=True),
        lax.all_gather(w_key, ("dp", "tp"), axis=0, tiled=True),
        lax.all_gather(w_value, ("dp", "tp"), axis=0, tiled=True),
        lax.all_gather(w_output, ("dp", "tp"), axis=0, tiled=True),
        lax.all_gather(gain_attention, ("dp", "tp"), axis=0, tiled=True),
        lax.all_gather(gain_feed, ("dp", "tp"), axis=0, tiled=True),
    )
    expand_full, reduce_full = (
        lax.all_gather(w_expand, "dp", axis=0, tiled=True),
        lax.all_gather(w_reduce, "dp", axis=1, tiled=True),
    )
    gain_one = gain_one.astype(jnp.float32)
    gain_two = gain_two.astype(jnp.float32)
    unit_one, scale_one = normalize(inputs)
    normed = (unit_one * gain_one).astype(jnp.bfloat16)
    query_rows = dot_plain(normed, query_full).astype(jnp.bfloat16)
    key_rows = dot_plain(normed, key_full).astype(jnp.bfloat16)
    value_rows = dot_plain(normed, value_full).astype(jnp.bfloat16)
    head_segments = jnp.repeat(segments, HEADS, axis=0)
    query_heads = split_heads(query_rows, rows_dev, pack_len)
    key_heads = split_heads(key_rows, rows_dev, pack_len)
    value_heads = split_heads(value_rows, rows_dev, pack_len)
    mixed_heads, row_maxima, row_sums = lax.map(
        head_forward, (query_heads, key_heads, value_heads, head_segments)
    )
    mixed_rows = merge_heads(mixed_heads, rows_dev, pack_len)
    branch = dot_plain(mixed_rows, output_full)
    middle = inputs + branch
    unit_two, scale_two = normalize(middle)
    normed_feed = (unit_two * gain_two).astype(jnp.bfloat16)
    normed_rows = lax.all_gather(normed_feed, "tp", axis=0, tiled=True)
    hidden = dot_plain(normed_rows, expand_full)
    gelu_value, gelu_pull = jax.vjp(partial(jax.nn.gelu, approximate=False), hidden)
    active = gelu_value.astype(jnp.bfloat16)
    feed_out = lax.psum_scatter(
        dot_plain(
            lax.slice_in_dim(active, 0, token_count * lax.axis_size("tp"), axis=0), reduce_full
        ),
        "tp",
        scatter_dimension=0,
        tiled=True,
    )
    result = (middle + feed_out).astype(jnp.bfloat16).reshape(rows_dev, pack_len, width)
    totals_all = lax.psum(
        (
            jnp.sum(inputs * inputs * valid_column),
            jnp.sum(branch * branch * valid_column),
            jnp.sum(feed_out * feed_out * valid_column),
            jnp.sum(valid_rows),
        ),
        ("dp", "tp"),
    )
    rms_stats = jnp.sqrt(jnp.stack(totals_all[:3]) / (totals_all[3] * width))
    grad_result = out_grad.reshape(token_count, width).astype(jnp.float32) * valid_column
    grad_feed = grad_result.astype(jnp.bfloat16)
    grad_rows = lax.all_gather(grad_feed, "tp", axis=0, tiled=True)
    grad_reduce = dot_first(active, grad_rows)
    grad_active = dot_last(grad_rows, reduce_full)
    grad_hidden = gelu_pull(grad_active)[0].astype(jnp.bfloat16)
    grad_expand = dot_first(normed_rows, grad_hidden)
    grad_normed_feed = lax.psum_scatter(
        dot_last(grad_hidden, expand_full), "tp", scatter_dimension=0, tiled=True
    )
    grad_norm_two, grad_gain_two = norm_back(grad_normed_feed, unit_two, scale_two, gain_two)
    grad_middle = grad_result + grad_norm_two
    grad_branch = grad_middle.astype(jnp.bfloat16)
    grad_output_w = dot_first(mixed_rows, grad_branch)
    grad_mixed = dot_last(grad_branch, output_full).astype(jnp.bfloat16)
    grad_heads = split_heads(grad_mixed, rows_dev, pack_len)
    grad_query_heads, grad_key_heads, grad_value_heads = lax.map(
        head_backward,
        (query_heads, key_heads, value_heads, head_segments, row_maxima, row_sums, grad_heads),
    )
    grad_query = merge_heads(grad_query_heads, rows_dev, pack_len)
    grad_key = merge_heads(grad_key_heads, rows_dev, pack_len)
    grad_value = merge_heads(grad_value_heads, rows_dev, pack_len)
    grad_query_w = dot_first(normed, grad_query)
    grad_key_w = dot_first(normed, grad_key)
    grad_value_w = dot_first(normed, grad_value)
    grad_normed = (
        dot_last(grad_query, query_full)
        + dot_last(grad_key, key_full)
        + dot_last(grad_value, value_full)
    )
    grad_norm_one, grad_gain_one = norm_back(grad_normed, unit_one, scale_one, gain_one)
    grad_inputs = (grad_middle + grad_norm_one).reshape(rows_dev, pack_len, width)
    shard_expand, shard_reduce = (
        lax.psum_scatter(grad_expand, "dp", scatter_dimension=0, tiled=True),
        lax.psum_scatter(grad_reduce, "dp", scatter_dimension=1, tiled=True),
    )
    shard_query, shard_key, shard_value, shard_output, shard_gain_one, shard_gain_two = (
        lax.psum_scatter(grad_query_w, ("dp", "tp"), scatter_dimension=0, tiled=True),
        lax.psum_scatter(grad_key_w, ("dp", "tp"), scatter_dimension=0, tiled=True),
        lax.psum_scatter(grad_value_w, ("dp", "tp"), scatter_dimension=0, tiled=True),
        lax.psum_scatter(grad_output_w, ("dp", "tp"), scatter_dimension=0, tiled=True),
        lax.psum_scatter(grad_gain_one, ("dp", "tp"), scatter_dimension=0, tiled=True),
        lax.psum_scatter(grad_gain_two, ("dp", "tp"), scatter_dimension=0, tiled=True),
    )
    return (
        result,
        grad_inputs,
        shard_query,
        shard_key,
        shard_value,
        shard_output,
        shard_gain_one,
        shard_gain_two,
        shard_expand,
        shard_reduce,
        rms_stats,
    )


def solution(mesh):
    in_specs = (
        P(("dp", "tp"), None, None),
        P(("dp", "tp"), None),
        P(("dp", "tp"), None, None),
        P(("dp", "tp"), None),
        P(("dp", "tp"), None),
        P(("dp", "tp"), None),
        P(("dp", "tp"), None),
        P(("dp", "tp")),
        P(("dp", "tp")),
        P("dp", "tp"),
        P("tp", "dp"),
    )
    out_specs = (
        P(("dp", "tp"), None, None),
        P(("dp", "tp"), None, None),
        P(("dp", "tp"), None),
        P(("dp", "tp"), None),
        P(("dp", "tp"), None),
        P(("dp", "tp"), None),
        P(("dp", "tp")),
        P(("dp", "tp")),
        P("dp", "tp"),
        P("tp", "dp"),
        P(),
    )
    return jax.shard_map(
        on_device, mesh=mesh, in_specs=in_specs, out_specs=out_specs, check_vma=False
    )
```

profile of v0, /device:TPU:0, one launch (start us, length us, event | category | flops | bytes accessed | tf_op | source)
XLA Modules:
  0.0 1258.4 jit_solution(7682637012286789652)
XLA Ops:
  13.2 42.1 %all-reduce.5 = (bf16[768]{0:T(1024)(128)(2,1)S(1)}, bf16[768]{0:T(1024)(128)(2,1)S(1)}) all-reduce(bf16[768]{0:T(1024)(128)(2,1)S(1)} %dynamic-update-slice, bf16[768]{0:T(1024)(128)(2,1)S(1)} %dynamic-update-slice.1), channel_id=1, replica_groups=mesh['dp'=8,'tp'=4] {'dp','tp'}, use_global_device_ids=true, to_apply=%add | all-reduce | flops 1536 | bytes 6144
  56.0 11.7 all-gather.9.cloned.1.call-done
  67.8 2.8 convolution_convert_fusion.3
  70.6 2.7 copy.43
  73.3 50.4 %all-gather.11.cloned.1.call-done = bf16[768,768]{1,0:T(8,128)(2,1)} async-done(((bf16[24,768]{1,0:T(8,128)(2,1)}), bf16[768,768]{1,0:T(8,128)(2,1)}) %all-gather.11.cloned.1.call-update) | async-done | bytes 1179664 | tf_op jit(solution)/shard_map/all_gather | solution.py:122
  123.7 2.8 convolution_convert_fusion.2
  126.5 2.8 copy.44
  129.2 50.3 %all-gather.13.cloned.1.call-done = bf16[768,768]{1,0:T(8,128)(2,1)} async-done(((bf16[24,768]{1,0:T(8,128)(2,1)}), bf16[768,768]{1,0:T(8,128)(2,1)}) %all-gather.13.cloned.1.call-update) | async-done | bytes 1179664 | tf_op jit(solution)/shard_map/all_gather | solution.py:123
  179.6 2.8 convolution_convert_fusion.1
  182.4 2.8 copy.45
  185.4 68.7 %while.28 = (s32[]{:T(128)}, bf16[12,1024,64]{1,2,0:T(8,128)(2,1)S(1)}, f32[12,1024,1]{1,2,0:T(1,128)}, f32[12,1024,1]{1,2,0:T(1,128)}, s32[12,1024]{1,0:T(8,128...) while((s32[]{:T(128)}, ...), condition=%wide.region_7.8_spmd, body=%wide.region_4.7_spmd.sunk | while | flops 284227584 | bytes 13568109 | solution.py:143
  254.2 5.0 fusion.102
  265.7 11.7 all-gather.19.cloned.1.call-done
  277.4 47.2 %all-gather.17.cloned.1.call-done = bf16[4096,768]{0,1:T(8,128)(2,1)} async-done(((bf16[1024,768]{0,1:T(8,128)(2,1)}), bf16[4096,768]{0,1:T(8,128)(2,1)}) %all-gather.17.cloned.1.call-update) | async-done | bytes 6291472 | tf_op jit(solution)/shard_map/all_gather | solution.py:151
  324.5 10.2 fusion.104
  334.7 33.1 %all-gather.21.cloned.1.call-done = bf16[768,768]{0,1:T(8,128)(2,1)} async-done(((bf16[768,96]{0,1:T(8,128)(2,1)}), bf16[768,768]{0,1:T(8,128)(2,1)}) %all-gather.21.cloned.1.call-update) | async-done | bytes 1179664 | tf_op jit(solution)/shard_map/all_gather | solution.py:130
  367.8 46.7 %all-gather.23.cloned.1.call-done = bf16[4096,768]{0,1:T(8,128)(2,1)} async-done(((bf16[1024,768]{0,1:T(8,128)(2,1)}), bf16[4096,768]{0,1:T(8,128)(2,1)}) %all-gather.23.cloned.1.call-update) | async-done | bytes 6291472 | tf_op jit(solution)/shard_map/all_gather | solution.py:176
  414.6 36.4 %add_convert_fusion = (bf16[4096,768]{1,0:T(8,128)(2,1)S(1)}, f32[4096,768]{1,0:T(8,128)}) fusion(f32[4096,768]{1,0:T(8,128)} %fusion.104, bf16[4096,768]{0,1:T(8,128)(2,1)} %all-gather.23.cloned.1.call-done, bf16[768,768]{0,1:T(8,128)(2,1)} %all-gather.21.cloned.1.call-done), kind=kOutput, calls=%fused_computation.64 | convolution fusion | flops 5058330624 | bytes 38928384 | tf_op jit(solution)/shard_map/dot_general | solution.py:51
  450.9 2.6 copy-done.40
  453.5 8.0 fusion.106
  461.6 11.3 multiply_convert_fusion.1
  472.9 3.7 copy-done.10
  476.6 7.9 fusion.105
  484.6 10.4 fusion.107
  495.1 10.1 fusion.110
  505.3 55.4 %reduce-scatter.11.cloned.1.call-done = f32[1024,768]{0,1:T(8,128)} async-done(((f32[4096,768]{0,1:T(8,128)}), f32[1024,768]{0,1:T(8,128)}) %reduce-scatter.11.cloned.1.call-update) | async-done | bytes 3145744 | tf_op jit(solution)/shard_map/reduce_scatter | solution.py:181
  560.7 2.9 multiply_reduce_fusion.3
  563.6 98.6 %reduce-scatter.9.cloned.1.call-done = f32[1024,768]{0,1:T(8,128)} async-done(((f32[4096,768]{0,1:T(8,128)}), f32[1024,768]{0,1:T(8,128)}) %reduce-scatter.9.cloned.1.call-update) | async-done | bytes 3145744 | tf_op jit(solution)/shard_map/reduce_scatter | solution.py:155
  662.3 6.7 multiply_reduce_fusion.2
  670.6 2.8 copy.49
  676.3 160.4 %while.29 = (s32[]{:T(128)}, bf16[12,1024,64]{1,2,0:T(8,128)(2,1)S(1)}, bf16[12,1024,64]{1,2,0:T(8,128)(2,1)}, bf16[12,1024,64]{1,2,0:T(8,128)(2,1)}, s32[12,102...) while((s32[]{:T(128)}, ...), condition=%wide.region_16.17_spmd, body=%wide.region_14.16_spmd.sunk | while | flops 682949632 | bytes 33739908 | solution.py:190
  679.6 2.7 multiply_reduce_fusion.9
  693.0 2.7 multiply_reduce_fusion.9
  706.3 2.7 multiply_reduce_fusion.9
  711.7 2.4 fusion.171
  714.1 2.4 fusion.172
  719.7 2.8 multiply_reduce_fusion.9
  733.1 2.7 multiply_reduce_fusion.9
  746.4 2.7 multiply_reduce_fusion.9
  759.8 2.7 multiply_reduce_fusion.9
  765.2 2.4 fusion.171
  767.6 2.4 fusion.172
  773.2 2.7 multiply_reduce_fusion.9
  786.5 2.7 multiply_reduce_fusion.9
  791.9 2.4 fusion.171
  799.9 2.7 multiply_reduce_fusion.9
  807.6 2.4 fusion.172
  813.2 2.7 multiply_reduce_fusion.9
  826.6 2.7 multiply_reduce_fusion.9
  834.3 2.4 fusion.172
  836.7 2.9 fusion.96
  839.7 4.3 fusion.94
  844.0 4.5 fusion.92
  848.6 4.8 fusion.86
  856.6 3.3 fusion.108
  861.7 2.9 fusion.75
  864.6 2.7 fusion.74
  867.3 3.6 copy.51
  870.8 39.8 %all-reduce.4 = (f32[768]{0:T(1024)S(1)}, f32[768]{0:T(1024)S(1)}, f32[1]{0:T(128)}, f32[1]{0:T(128)}, f32[1]{0:T(128)}, /*index=5*/f32[]{:T(128)}) all-reduce(f32[768]{0:T(1024)S(1)} %get-tuple-element.155, f32[768]{0:T(1024)S(1)} %get-tuple-element.153, f32[1]{0:T(128)} %bitcast.60, ...), channel_id=8, replica_groups=mesh['dp'=8,'tp'=4] {'dp','tp'}, use_global_device_ids=true, to_apply=%region_24.25.clone | all-reduce | flops 1540 | bytes 12320
  912.4 2.4 fusion.90
  914.8 23.9 %reduce-scatter.13.cloned.1.call-done = f32[24,768]{1,0:T(8,128)} async-done(((f32[768,768]{1,0:T(8,128)}), f32[24,768]{1,0:T(8,128)}) %reduce-scatter.13.cloned.1.call-update) | async-done | bytes 73744 | tf_op jit(solution)/shard_map/reduce_scatter | solution.py:212
  938.7 104.6 %reduce-scatter.15.cloned.1.call-done = f32[24,768]{1,0:T(8,128)} async-done(((f32[768,768]{1,0:T(8,128)}), f32[24,768]{1,0:T(8,128)}) %reduce-scatter.15.cloned.1.call-update) | async-done | bytes 73744 | tf_op jit(solution)/shard_map/reduce_scatter | solution.py:213
  1043.3 103.7 %reduce-scatter.17.cloned.1.call-done = f32[24,768]{1,0:T(8,128)} async-done(((f32[768,768]{1,0:T(8,128)}), f32[24,768]{1,0:T(8,128)}) %reduce-scatter.17.cloned.1.call-update) | async-done | bytes 73744 | tf_op jit(solution)/shard_map/reduce_scatter | solution.py:214
  1147.0 104.7 %reduce-scatter.19.cloned.1.call-done = f32[24,768]{1,0:T(8,128)} async-done(((f32[768,768]{1,0:T(8,128)}), f32[24,768]{1,0:T(8,128)}) %reduce-scatter.19.cloned.1.call-update) | async-done | bytes 73744 | tf_op jit(solution)/shard_map/reduce_scatter | solution.py:215
  (288 shorter events, 203.3 us)
Async XLA Ops:
  7.2 5.2 copy-start.37
  7.2 5.5 copy-start.38
  7.2 5.8 copy-start.39
  7.2 60.6 %all-gather.9.cloned.1.call-start = ((), (), s32[]{:S(2)}) async-start(), calls=%async_computation.8 | async-start | bytes 1216512 | tf_op jit(solution)/shard_map/all_gather | solution.py:121
  7.9 115.7 %all-gather.11.cloned.1.call-start = ((), (), s32[]{:S(2)}) async-start(), calls=%async_computation.9 | async-start | bytes 1216512 | tf_op jit(solution)/shard_map/all_gather | solution.py:122
  8.7 170.9 %all-gather.13.cloned.1.call-start = ((), (), s32[]{:S(2)}) async-start(), calls=%async_computation.10 | async-start | bytes 1216512 | tf_op jit(solution)/shard_map/all_gather | solution.py:123
  9.4 244.7 %all-gather.15.cloned.1.call-start = ((), (), s32[]{:S(2)}) async-start(), calls=%async_computation.11 | async-start | bytes 1216512 | tf_op jit(solution)/shard_map/all_gather | solution.py:124
  10.0 267.4 %all-gather.19.cloned.1.call-start = ((), (), s32[]{:S(2)}) async-start(), calls=%async_computation.13 | async-start | bytes 1327104 | tf_op jit(solution)/shard_map/all_gather | solution.py:129
  10.6 314.0 %all-gather.17.cloned.1.call-start = ((), (), s32[]{:S(2)}) async-start(), calls=%async_computation.12 | async-start | bytes 7864320 | tf_op jit(solution)/shard_map/all_gather | solution.py:151
  12.4 241.8 %copy-start.2 = (bf16[1,1024,768]{1,2,0:T(8,128)(2,1)}, bf16[1,1024,768]{1,2,0:T(8,128)(2,1)S(1)}, u32[]{:S(2)}) copy-start(bf16[1,1024,768]{1,2,0:T(8,128)(2,1)S(1)} %copy.42) | copy-start | bytes 4718596
  12.7 251.3 %copy-start.19 = (s32[1024]{0:T(1024)}, s32[1024]{0:T(1024)S(1)}, u32[]{:S(2)}) copy-start(s32[1024]{0:T(1024)S(1)} %fusion.89) | copy-start | bytes 12292
  55.2 124.3 %copy-start.29 = (f32[768]{0:T(1024)}, f32[768]{0:T(1024)S(1)}, u32[]{:S(2)}) copy-start(f32[768]{0:T(1024)S(1)} %convert_element_type.106) | copy-start | bytes 9220
  55.5 124.0 %copy-start.25 = (f32[1024]{0:T(1024)}, f32[1024]{0:T(1024)S(1)}, u32[]{:S(2)}) copy-start(f32[1024]{0:T(1024)S(1)} %broadcast_multiply_fusion.5) | copy-start | bytes 12292
  56.0 123.6 %copy-start.31 = (f32[1024]{0:T(1024)}, f32[1024]{0:T(1024)S(1)}, u32[]{:S(2)}) copy-start(f32[1024]{0:T(1024)S(1)} %add_rsqrt_fusion.1) | copy-start | bytes 12292
  56.0 203.5 %copy-start.21 = (f32[768]{0:T(1024)}, f32[768]{0:T(1024)S(1)}, u32[]{:S(2)}) copy-start(f32[768]{0:T(1024)S(1)} %convert_element_type.111) | copy-start | bytes 9220
  254.1 5.0 copy-start.7
  254.1 5.0 copy-start.16
  259.1 1.7 copy-start
  259.1 1.7 copy-start.17
  260.8 1.6 copy-start.23
  260.8 2.4 copy-start.11
  262.4 105.5 %all-gather.21.cloned.1.call-start = ((), (), s32[]{:S(2)}) async-start(), calls=%async_computation.14 | async-start | bytes 1327104 | tf_op jit(solution)/shard_map/all_gather | solution.py:130
  263.1 151.4 %all-gather.23.cloned.1.call-start = ((), (), s32[]{:S(2)}) async-start(), calls=%async_computation.16 | async-start | bytes 7864320 | tf_op jit(solution)/shard_map/all_gather | solution.py:176
  263.9 70.8 %copy-start.4 = (bf16[1,1024,768]{1,2,0:T(8,128)(2,1)}, bf16[1,1024,768]{1,2,0:T(8,128)(2,1)S(1)}, u32[]{:S(2)}) copy-start(bf16[1,1024,768]{1,2,0:T(8,128)(2,1)S(1)} %copy.47) | copy-start | bytes 4718596
  264.0 70.8 %copy-start.27 = (f32[1024]{0:T(1024)}, f32[1024]{0:T(1024)S(1)}, u32[]{:S(2)}) copy-start(f32[1024]{0:T(1024)S(1)} %compare_convert_fusion.1) | copy-start | bytes 12292
  265.6 295.1 %reduce-scatter.11.cloned.1.call-start = ((), (), s32[]{:S(2)}) async-start(), calls=%async_computation.17 | async-start | bytes 15728640 | tf_op jit(solution)/shard_map/reduce_scatter | solution.py:181
  334.7 118.8 %copy-start.35 = (bf16[768,768]{1,0:T(8,128)(2,1)S(1)}, bf16[768,768]{1,0:T(8,128)(2,1)}, u32[]{:S(2)}) copy-start(bf16[768,768]{1,0:T(8,128)(2,1)} %all-gather.19.cloned.1.call-done) | copy-start | bytes 3538948
  450.9 2.6 copy-start.40
  461.5 200.7 %reduce-scatter.9.cloned.1.call-start = ((), (), s32[]{:S(2)}) async-start(), calls=%async_computation.15 | async-start | bytes 15728640 | tf_op jit(solution)/shard_map/reduce_scatter | solution.py:155
  461.6 15.1 %copy-start.36 = (bf16[768,768]{0,1:T(8,128)(2,1)S(1)}, bf16[768,768]{0,1:T(8,128)(2,1)}, u32[]{:S(2)}) copy-start(bf16[768,768]{0,1:T(8,128)(2,1)} %all-gather.21.cloned.1.call-done) | copy-start | bytes 3538948
  472.9 3.8 copy-start.10
  484.6 430.2 %reduce-scatter.21.cloned.1.call-start = ((), (), s32[]{:S(2)}) async-start(), calls=%async_computation.22 | async-start | bytes 2654208 | tf_op jit(solution)/shard_map/reduce_scatter | solution.py:208
  495.1 65.7 %copy-start.18 = (f32[1024]{0:T(1024)S(1)}, f32[1024]{0:T(1024)}, u32[]{:S(2)}) copy-start(f32[1024]{0:T(1024)} %copy-done.17) | copy-start | bytes 12292
  495.1 65.7 %copy-start.22 = (f32[768]{0:T(1024)S(1)}, f32[768]{0:T(1024)}, u32[]{:S(2)}) copy-start(f32[768]{0:T(1024)} %copy-done.21) | copy-start | bytes 9220
  495.1 65.7 %copy-start.24 = (f32[1024]{0:T(1024)S(1)}, f32[1024]{0:T(1024)}, u32[]{:S(2)}) copy-start(f32[1024]{0:T(1024)} %copy-done.23) | copy-start | bytes 12292
  495.1 419.7 %reduce-scatter.23.cloned.1.call-start = ((), (), s32[]{:S(2)}) async-start(), calls=%async_computation.23 | async-start | bytes 2654208 | tf_op jit(solution)/shard_map/reduce_scatter | solution.py:209
  495.1 65.6 %copy-start.1 = (f32[1024,768]{0,1:T(8,128)S(1)}, f32[1024,768]{0,1:T(8,128)}, u32[]{:S(2)}) copy-start(f32[1024,768]{0,1:T(8,128)} %copy-done) | copy-start | bytes 9437188
  505.3 157.0 %copy-start.28 = (f32[1024]{0:T(1024)S(1)}, f32[1024]{0:T(1024)}, u32[]{:S(2)}) copy-start(f32[1024]{0:T(1024)} %copy-done.27) | copy-start | bytes 12292
  505.3 433.4 %reduce-scatter.13.cloned.1.call-start = ((), (), s32[]{:S(2)}) async-start(), calls=%async_computation.18 | async-start | bytes 2433024 | tf_op jit(solution)/shard_map/reduce_scatter | solution.py:212
  662.3 6.7 copy-start.15
  668.9 1.7 copy-start.5
  676.3 160.4 %copy-start.3 = (bf16[1,1024,768]{1,2,0:T(8,128)(2,1)S(1)}, bf16[1,1024,768]{1,2,0:T(8,128)(2,1)}, u32[]{:S(2)}) copy-start(bf16[1,1024,768]{1,2,0:T(8,128)(2,1)} %copy-done.2) | copy-start | bytes 4718596
  676.3 160.4 %copy-start.26 = (f32[1024]{0:T(1024)S(1)}, f32[1024]{0:T(1024)}, u32[]{:S(2)}) copy-start(f32[1024]{0:T(1024)} %copy-done.25) | copy-start | bytes 12292
  676.3 160.4 %copy-start.30 = (f32[768]{0:T(1024)S(1)}, f32[768]{0:T(1024)}, u32[]{:S(2)}) copy-start(f32[768]{0:T(1024)} %copy-done.29) | copy-start | bytes 9220
  676.3 160.4 %copy-start.32 = (f32[1024]{0:T(1024)S(1)}, f32[1024]{0:T(1024)}, u32[]{:S(2)}) copy-start(f32[1024]{0:T(1024)} %copy-done.31) | copy-start | bytes 12292
  836.7 2.9 copy-start.12
  839.6 203.7 %reduce-scatter.15.cloned.1.call-start = ((), (), s32[]{:S(2)}) async-start(), calls=%async_computation.19 | async-start | bytes 2433024 | tf_op jit(solution)/shard_map/reduce_scatter | solution.py:213
  844.0 303.0 %reduce-scatter.17.cloned.1.call-start = ((), (), s32[]{:S(2)}) async-start(), calls=%async_computation.20 | async-start | bytes 2433024 | tf_op jit(solution)/shard_map/reduce_scatter | solution.py:214
  844.0 4.6 copy-start.8
  848.6 4.9 copy-start.20
  848.6 403.1 %reduce-scatter.19.cloned.1.call-start = ((), (), s32[]{:S(2)}) async-start(), calls=%async_computation.21 | async-start | bytes 2433024 | tf_op jit(solution)/shard_map/reduce_scatter | solution.py:215
  853.4 1.4 copy-start.9
  856.6 3.3 copy-start.13
  856.6 3.3 copy-start.33
  859.9 1.4 copy-start.14
  859.9 1.8 copy-start.34
  861.7 2.9 copy-start.6
Sparse Core Ops, SparseCore 0:
  10.9 56.7 all-gather.8
  70.7 52.9 all-gather.10
  126.6 52.9 all-gather.12
  182.3 52.9 all-gather.14
  237.4 39.9 all-gather.18
  279.4 45.1 all-gather.16
  326.7 41.0 all-gather.20
  369.4 45.1 all-gather.22
  461.6 99.0 reduce-scatter.10
  563.2 99.0 reduce-scatter.8
  666.3 68.9 reduce-scatter.20
  739.3 68.2 reduce-scatter.22
  839.7 98.9 reduce-scatter.12
  945.3 97.9 reduce-scatter.14
  1049.1 97.9 reduce-scatter.16
  1153.6 98.0 reduce-scatter.18
where the time goes:
time: 1270 us; the launch traced here: 1260 us
  waiting for transfers between devices  746 us (59%)
  matrix products  299 us (24%)
  blocking collectives  81.8 us (6%)
  local copies, waits for them, and re-layouts  57.7 us (5%)
  other arithmetic  57.1 us (4%)
  between operations  15.3 us (1%)
    dot_general x42, matrix products, dot_last(): lax.dot_general(left_side, right_side, (((1,), (1,)), ((), ())), preferre...  128 us
    reduce_scatter x1, waiting for transfers between devices, on_device(): lax.psum_scatter(grad_output_w, ('dp', 'tp'), scatter_dimension=0, tiled=...  105 us
    reduce_scatter x1, waiting for transfers between devices, on_device(): lax.psum_scatter(grad_key_w, ('dp', 'tp'), scatter_dimension=0, tiled=True)  105 us
    reduce_scatter x1, waiting for transfers between devices, on_device(): lax.psum_scatter(grad_value_w, ('dp', 'tp'), scatter_dimension=0, tiled=T...  104 us
    reduce_scatter x1, waiting for transfers between devices, on_device(): lax.psum_scatter(dot_plain(lax.slice_in_dim(active, 0, token_count * lax....  98.6 us
    dot_general x30, matrix products, dot_first(): lax.dot_general(left_side, right_side, (((0,), (0,)), ((), ())), preferre...  94.1 us
    unnamed x2, blocking collectives  81.8 us
    dot_general x30, matrix products, dot_plain(): return jnp.dot(left_side, right_side, preferred_element_type=jnp.float32)  76.9 us
  transfers between devices with their start and end apart: 16, of which 13 were waited for; matrix products, arithmetic and copies ran while one was open for 29% of the time, Pallas kernels for 0%

commit v1 on v0

--- a/solution.py
+++ b/solution.py
@@ -1,3 +1,4 @@
+import functools
 from functools import partial
 import jax
 import jax.numpy as jnp
@@ -7,6 +8,25 @@
 HEADS = 12
 HEAD_DIM = 64
 SLOTS = 4
+
+
+def report_roads(state, group_axis):
+    shares = jax.lax.axis_size(group_axis)
+    series = []
+    for k0 in [*range(1, shares)]:
+        series.append((k0 - 1, k0))
+    big = series + [(shares - 1, 0)]
+    side_arr = state
+    leaves = [side_arr]
+    for _ in tuple(range(shares - 1)):
+        side_arr = jax.lax.ppermute(side_arr, axis_name=group_axis, perm=big)
+        leaves += [side_arr]
+    f_now = jnp.concatenate([*reversed(leaves)], axis=0)
+    z = jax.lax.axis_index(group_axis)
+    return jnp.roll(f_now, (z + 1) * side_arr.shape[0], axis=0)
+
+
+test_body = functools.partial(report_roads, group_axis="tp")
 
 
 def segment_numbers(lengths, pack_len):
@@ -173,7 +193,7 @@
     rms_stats = jnp.sqrt(jnp.stack(totals_all[:3]) / (totals_all[3] * width))
     grad_result = out_grad.reshape(token_count, width).astype(jnp.float32) * valid_column
     grad_feed = grad_result.astype(jnp.bfloat16)
-    grad_rows = lax.all_gather(grad_feed, "tp", axis=0, tiled=True)
+    grad_rows = test_body(grad_feed)
     grad_reduce = dot_first(active, grad_rows)
     grad_active = dot_last(grad_rows, reduce_full)
     grad_hidden = gelu_pull(grad_active)[0].astype(jnp.bfloat16)

time: 1270 us -> 1220 us (0.961)
  waiting for transfers between devices: 746 us -> 664 us
  matrix products: 299 us -> 314 us
  local copies, waits for them, and re-layouts: 57.7 us -> 71.4 us
    reduce_scatter x1, waiting for transfers between devices: 105 us -> 0.01 us  [on_device(): lax.psum_scatter(grad_output_w, ('dp', 'tp'), scatter_dimension=0, tiled=...]
    ppermute x0 -> x3, waiting for transfers between devices: none -> 87.5 us  [report_roads(): side_arr = jax.lax.ppermute(side_arr, axis_name=group_axis, perm=big)]
    reduce_scatter x1, waiting for transfers between devices: 23.9 us -> 94.3 us  [on_device(): lax.psum_scatter(grad_query_w, ('dp', 'tp'), scatter_dimension=0, tiled=T...]
    all_gather x1, waiting for transfers between devices: 47.2 us -> 0.01 us  [on_device(): normed_rows = lax.all_gather(normed_feed, 'tp', axis=0, tiled=True)]
    all_gather x1 -> x0, waiting for transfers between devices: 46.7 us -> none  [on_device(): grad_rows = lax.all_gather(grad_feed, 'tp', axis=0, tiled=True)]
    all_gather x1, waiting for transfers between devices: 50.3 us -> 9.91 us  [on_device(): lax.all_gather(w_value, ('dp', 'tp'), axis=0, tiled=True)]
    all_gather x1, waiting for transfers between devices: 11.7 us -> 50.3 us  [on_device(): lax.all_gather(w_query, ('dp', 'tp'), axis=0, tiled=True)]
    dot_general x30, matrix products: 76.9 us -> 114 us  [dot_plain(): return jnp.dot(left_side, right_side, preferred_element_type=jnp.float32)]
  transfers between devices with their start and end apart: 16 -> 18, of which waited for: 13 -> 11; matrix products, arithmetic and copies ran while one was open for 29% -> 34% of each run, Pallas kernels for 0% -> 0%
where the time goes in v1:
time: 1220 us; the launch traced here: 1200 us
  waiting for transfers between devices  664 us (54%)
  matrix products  314 us (26%)
  blocking collectives  81.8 us (7%)
  local copies, waits for them, and re-layouts  71.4 us (6%)
  other arithmetic  51.4 us (4%)
  between operations  15.5 us (1%)
    dot_general x30, matrix products, dot_plain(): return jnp.dot(left_side, right_side, preferred_element_type=jnp.float32)  114 us
    dot_general x42, matrix products, dot_last(): lax.dot_general(left_side, right_side, (((1,), (1,)), ((), ())), preferre...  112 us
    reduce_scatter x1, waiting for transfers between devices, on_device(): lax.psum_scatter(grad_value_w, ('dp', 'tp'), scatter_dimension=0, tiled=T...  105 us
    reduce_scatter x1, waiting for transfers between devices, on_device(): lax.psum_scatter(grad_key_w, ('dp', 'tp'), scatter_dimension=0, tiled=True)  104 us
    reduce_scatter x1, waiting for transfers between devices, on_device(): lax.psum_scatter(dot_plain(lax.slice_in_dim(active, 0, token_count * lax....  98.8 us
    reduce_scatter x1, waiting for transfers between devices, on_device(): lax.psum_scatter(grad_query_w, ('dp', 'tp'), scatter_dimension=0, tiled=T...  94.3 us
    dot_general x30, matrix products, dot_first(): lax.dot_general(left_side, right_side, (((0,), (0,)), ((), ())), preferre...  88.2 us
    ppermute x3, waiting for transfers between devices, report_roads(): side_arr = jax.lax.ppermute(side_arr, axis_name=group_axis, perm=big)  87.5 us
  transfers between devices with their start and end apart: 18, of which 11 were waited for; matrix products, arithmetic and copies ran while one was open for 34% of the time, Pallas kernels for 0%

profile of v1, /device:TPU:0, one launch (start us, length us, event | category | flops | bytes accessed | tf_op | source)
XLA Modules:
  0.0 1202.6 jit_solution(17534641357590016185)
XLA Ops:
  13.1 42.1 %all-reduce.5 = (bf16[768]{0:T(1024)(128)(2,1)S(1)}, bf16[768]{0:T(1024)(128)(2,1)S(1)}) all-reduce(bf16[768]{0:T(1024)(128)(2,1)S(1)} %dynamic-update-slice, bf16[768]{0:T(1024)(128)(2,1)S(1)} %dynamic-update-slice.1), channel_id=1, replica_groups=mesh['dp'=8,'tp'=4] {'dp','tp'}, use_global_device_ids=true, to_apply=%add | all-reduce | flops 1536 | bytes 6144
  57.8 9.9 all-gather.12.cloned.1.call-done
  67.7 2.8 convolution_convert_fusion.1
  70.5 2.8 copy.45
  73.3 50.3 %all-gather.10.cloned.1.call-done = bf16[768,768]{1,0:T(8,128)(2,1)} async-done(((bf16[24,768]{1,0:T(8,128)(2,1)}), bf16[768,768]{1,0:T(8,128)(2,1)}) %all-gather.10.cloned.1.call-update) | async-done | bytes 1179664 | tf_op jit(solution)/shard_map/all_gather | solution.py:142
  123.6 2.8 convolution_convert_fusion.2
  126.4 2.8 copy.44
  129.2 50.3 %all-gather.8.cloned.1.call-done = bf16[768,768]{1,0:T(8,128)(2,1)} async-done(((bf16[24,768]{1,0:T(8,128)(2,1)}), bf16[768,768]{1,0:T(8,128)(2,1)}) %all-gather.8.cloned.1.call-update) | async-done | bytes 1179664 | tf_op jit(solution)/shard_map/all_gather | solution.py:141
  179.5 2.8 convolution_convert_fusion.3
  182.3 2.7 copy.43
  185.3 68.9 %while.28 = (s32[]{:T(128)}, bf16[12,1024,64]{1,2,0:T(8,128)(2,1)S(1)}, f32[12,1024,1]{1,2,0:T(1,128)}, f32[12,1024,1]{1,2,0:T(1,128)}, s32[12,1024]{1,0:T(8,128...) while((s32[]{:T(128)}, ...), condition=%wide.region_7.8_spmd, body=%wide.region_4.7_spmd.sunk | while | flops 284227584 | bytes 13568109 | solution.py:163
  254.3 5.0 fusion.110
  264.1 19.5 %collective-permute-done = bf16[1024,768]{0,1:T(8,128)(2,1)S(1)} collective-permute-done((bf16[1024,768]{0,1:T(8,128)(2,1)S(1)}, bf16[1024,768]{0,1:T(8,128)(2,1)S(1)}, u32[]{:S(2)}, u32[]{:S(2)}) %collective-permute-start) | collective-permute-done | bytes 1572896 | tf_op jit(solution)/shard_map/ppermute | solution.py:22
  283.7 48.6 %collective-permute-done.1 = bf16[1024,768]{0,1:T(8,128)(2,1)} collective-permute-done((bf16[1024,768]{0,1:T(8,128)(2,1)S(1)}, bf16[1024,768]{0,1:T(8,128)(2,1)}, u32[]{:S(2)}, u32[]{:S(2)}) %collective-permute-start.1) | collective-permute-done | bytes 1572896 | tf_op jit(solution)/shard_map/ppermute | solution.py:22
  332.3 2.5 collective-permute-start.2
  334.9 19.3 %collective-permute-done.2 = bf16[1024,768]{0,1:T(8,128)(2,1)} collective-permute-done((bf16[1024,768]{0,1:T(8,128)(2,1)}, bf16[1024,768]{0,1:T(8,128)(2,1)}, u32[]{:S(2)}, u32[]{:S(2)}) %collective-permute-start.2) | collective-permute-done | bytes 1572896 | tf_op jit(solution)/shard_map/ppermute | solution.py:22
  354.2 2.8 constant_dynamic-update-slice_fusion.9
  357.0 2.8 constant_dynamic-update-slice_fusion.8
  362.7 2.8 constant_dynamic-update-slice_fusion.5
  365.6 2.9 constant_dynamic-update-slice_fusion.4
  371.4 34.8 %multiply_convert_fusion.1 = (bf16[4096,768]{1,0:T(8,128)(2,1)}, f32[4096,768]{1,0:T(8,128)}, f32[4096,768]{1,0:T(8,128)}) fusion(bf16[4096,768]{0,1:T(8,128)(2,1)} %all-gather.16.cloned.1.call-done, bf16[768,768]{1,0:T(8,128)(2,1)} %all-gather.18.cloned.1.call-done), kind=kOutput, calls=%fused_computation.65 | convolution fusion | flops 5036310528 | bytes 38928384 | tf_op jit(solution)/shard_map/dot_general | solution.py:61
  406.2 16.9 %add_convert_fusion = bf16[4096,768]{1,0:T(8,128)(2,1)S(1)} fusion(f32[4096,768]{1,0:T(8,128)} %get-tuple-element.209, f32[4096,768]{1,0:T(8,128)} %get-tuple-element.223, bf16[768,768]{0,1:T(8,128)(2,1)} %all-gather.20.cloned.1.call-done, bf16[8192,768]{0,1:T(8,128)(2,1)} %constant_dynamic-update-slice_fusion.2, s32[]{:T(128)S(6)} %select_n.21), kind=kOutput, calls=%fused_computation.64 | convolution fusion | flops 4875878400 | bytes 38928388 | tf_op jit(solution)/shard_map/dot_general | solution.py:71
  423.1 2.6 copy-done.35
  425.7 7.9 fusion.113
  434.9 12.9 %fusion.112 = f32[4096,768]{0,1:T(8,128)} fusion(bf16[4096,768]{1,0:T(8,128)(2,1)} %get-tuple-element.208, bf16[768,768]{0,1:T(8,128)(2,1)S(1)} %copy-done.34), kind=kOutput, calls=%fused_computation.159 | convolution fusion | flops 4831838208 | bytes 20054016 | tf_op jit(solution)/shard_map/dot_general | solution.py:61
  447.8 11.3 fusion.114
  459.3 11.2 fusion.60
  470.5 61.2 %reduce-scatter.11.cloned.1.call-done = f32[1024,768]{0,1:T(8,128)} async-done(((f32[4096,768]{0,1:T(8,128)}), f32[1024,768]{0,1:T(8,128)}) %reduce-scatter.11.cloned.1.call-update) | async-done | bytes 3145744 | tf_op jit(solution)/shard_map/reduce_scatter | solution.py:201
  531.8 2.9 multiply_reduce_fusion.3
  534.7 98.8 %reduce-scatter.9.cloned.1.call-done = f32[1024,768]{0,1:T(8,128)} async-done(((f32[4096,768]{0,1:T(8,128)}), f32[1024,768]{0,1:T(8,128)}) %reduce-scatter.9.cloned.1.call-update) | async-done | bytes 3145744 | tf_op jit(solution)/shard_map/reduce_scatter | solution.py:175
  633.5 6.7 multiply_reduce_fusion.2
  640.1 2.6 convolution_convert_fusion
  642.7 4.3 copy.49
  647.0 4.3 fusion.92
  654.3 160.6 %while.29 = (s32[]{:T(128)}, bf16[12,1024,64]{1,2,0:T(8,128)(2,1)}, bf16[12,1024,64]{1,2,0:T(8,128)(2,1)}, bf16[12,1024,64]{1,2,0:T(8,128)(2,1)S(1)}, s32[12,102...) while((s32[]{:T(128)}, bf16[12,1024,64]{1,2,0:T(8,128)(2,1)}, ...), condition=%wide.region_16.17_spmd, body=%wide.region_14.16_spmd.sunk | while | flops 682949632 | bytes 33739908 | solution.py:210
  657.8 2.7 multiply_reduce_fusion.9
  663.5 2.4 fusion.175
  671.2 2.7 multiply_reduce_fusion.9
  676.8 2.4 fusion.175
  684.6 2.7 multiply_reduce_fusion.9
  697.9 2.7 multiply_reduce_fusion.9
  711.2 2.7 multiply_reduce_fusion.9
  724.6 2.7 multiply_reduce_fusion.9
  730.2 2.4 fusion.175
  737.9 2.7 multiply_reduce_fusion.9
  751.3 2.7 multiply_reduce_fusion.9
  756.9 2.4 fusion.175
  764.7 2.7 multiply_reduce_fusion.9
  778.1 2.7 multiply_reduce_fusion.9
  791.4 2.7 multiply_reduce_fusion.9
  797.0 2.4 fusion.175
  804.8 2.7 multiply_reduce_fusion.9
  814.9 4.9 fusion.104
  819.9 4.4 fusion.102
  824.3 2.9 fusion.100
  830.2 3.6 fusion.115
  835.6 4.3 fusion.79
  839.9 39.7 %all-reduce.4 = (f32[768]{0:T(1024)S(1)}, f32[768]{0:T(1024)S(1)}, f32[1]{0:T(128)}, f32[1]{0:T(128)}, f32[1]{0:T(128)}, /*index=5*/f32[]{:T(128)}) all-reduce(f32[768]{0:T(1024)S(1)} %get-tuple-element.155, f32[768]{0:T(1024)S(1)} %get-tuple-element.153, f32[1]{0:T(128)} %bitcast.60, ...), channel_id=8, replica_groups=mesh['dp'=8,'tp'=4] {'dp','tp'}, use_global_device_ids=true, to_apply=%region_24.25.clone | all-reduce | flops 1540 | bytes 12320
  880.8 5.5 fusion.78
  886.3 3.5 copy.51
  890.6 2.4 fusion.96
  893.0 94.3 %reduce-scatter.13.cloned.1.call-done = f32[24,768]{1,0:T(8,128)} async-done(((f32[768,768]{1,0:T(8,128)}), f32[24,768]{1,0:T(8,128)}) %reduce-scatter.13.cloned.1.call-update) | async-done | bytes 73744 | tf_op jit(solution)/shard_map/reduce_scatter | solution.py:232
  987.3 103.8 %reduce-scatter.15.cloned.1.call-done = f32[24,768]{1,0:T(8,128)} async-done(((f32[768,768]{1,0:T(8,128)}), f32[24,768]{1,0:T(8,128)}) %reduce-scatter.15.cloned.1.call-update) | async-done | bytes 73744 | tf_op jit(solution)/shard_map/reduce_scatter | solution.py:233
  1091.1 104.6 %reduce-scatter.17.cloned.1.call-done = f32[24,768]{1,0:T(8,128)} async-done(((f32[768,768]{1,0:T(8,128)}), f32[24,768]{1,0:T(8,128)}) %reduce-scatter.17.cloned.1.call-update) | async-done | bytes 73744 | tf_op jit(solution)/shard_map/reduce_scatter | solution.py:234
  (288 shorter events, 213.6 us)
Async XLA Ops:
  7.2 60.6 %all-gather.12.cloned.1.call-start = ((), (), s32[]{:S(2)}) async-start(), calls=%async_computation.10 | async-start | bytes 1216512 | tf_op jit(solution)/shard_map/all_gather | solution.py:143
  7.9 115.7 %all-gather.10.cloned.1.call-start = ((), (), s32[]{:S(2)}) async-start(), calls=%async_computation.9 | async-start | bytes 1216512 | tf_op jit(solution)/shard_map/all_gather | solution.py:142
  8.7 170.9 %all-gather.8.cloned.1.call-start = ((), (), s32[]{:S(2)}) async-start(), calls=%async_computation.8 | async-start | bytes 1216512 | tf_op jit(solution)/shard_map/all_gather | solution.py:141
  9.4 244.8 %all-gather.14.cloned.1.call-start = ((), (), s32[]{:S(2)}) async-start(), calls=%async_computation.11 | async-start | bytes 1216512 | tf_op jit(solution)/shard_map/all_gather | solution.py:144
  10.0 361.4 %all-gather.18.cloned.1.call-start = ((), (), s32[]{:S(2)}) async-start(), calls=%async_computation.13 | async-start | bytes 1327104 | tf_op jit(solution)/shard_map/all_gather | solution.py:149
  10.6 360.9 %all-gather.16.cloned.1.call-start = ((), (), s32[]{:S(2)}) async-start(), calls=%async_computation.12 | async-start | bytes 7864320 | tf_op jit(solution)/shard_map/all_gather | solution.py:171
  55.2 124.3 %copy-start.27 = (f32[768]{0:T(1024)}, f32[768]{0:T(1024)S(1)}, u32[]{:S(2)}) copy-start(f32[768]{0:T(1024)S(1)} %convert_element_type.106) | copy-start | bytes 9220
  55.3 208.0 %copy-start.19 = (s32[1024]{0:T(1024)}, s32[1024]{0:T(1024)S(1)}, u32[]{:S(2)}) copy-start(s32[1024]{0:T(1024)S(1)} %fusion.95) | copy-start | bytes 12292
  55.3 204.3 %copy-start.21 = (f32[768]{0:T(1024)}, f32[768]{0:T(1024)S(1)}, u32[]{:S(2)}) copy-start(f32[768]{0:T(1024)S(1)} %convert_element_type.111) | copy-start | bytes 9220
  57.0 197.2 %copy-start.2 = (bf16[1,1024,768]{1,2,0:T(8,128)(2,1)}, bf16[1,1024,768]{1,2,0:T(8,128)(2,1)S(1)}, u32[]{:S(2)}) copy-start(bf16[1,1024,768]{1,2,0:T(8,128)(2,1)S(1)} %copy.42) | copy-start | bytes 4718596
  57.3 122.2 %copy-start.25 = (f32[1024]{0:T(1024)}, f32[1024]{0:T(1024)S(1)}, u32[]{:S(2)}) copy-start(f32[1024]{0:T(1024)S(1)} %broadcast_multiply_fusion.5) | copy-start | bytes 12292
  57.8 121.7 %copy-start.29 = (f32[1024]{0:T(1024)}, f32[1024]{0:T(1024)S(1)}, u32[]{:S(2)}) copy-start(f32[1024]{0:T(1024)S(1)} %add_rsqrt_fusion.1) | copy-start | bytes 12292
  254.2 5.0 copy-start.7
  254.2 5.0 copy-start.14
  259.2 1.6 copy-start
  259.3 1.6 copy-start.17
  260.9 1.6 copy-start.23
  260.9 1.7 copy-start.9
  262.5 143.8 %all-gather.20.cloned.1.call-start = ((), (), s32[]{:S(2)}) async-start(), calls=%async_computation.14 | async-start | bytes 1327104 | tf_op jit(solution)/shard_map/all_gather | solution.py:150
  263.3 106.5 %copy-start.4 = (bf16[1,1024,768]{1,2,0:T(8,128)(2,1)}, bf16[1,1024,768]{1,2,0:T(8,128)(2,1)S(1)}, u32[]{:S(2)}) copy-start(bf16[1,1024,768]{1,2,0:T(8,128)(2,1)S(1)} %copy.47) | copy-start | bytes 4718596
  263.3 106.5 %copy-start.15 = (f32[1024]{0:T(1024)}, f32[1024]{0:T(1024)S(1)}, u32[]{:S(2)}) copy-start(f32[1024]{0:T(1024)S(1)} %compare_convert_fusion.1) | copy-start | bytes 12292
  263.8 19.9 %collective-permute-start = (bf16[1024,768]{0,1:T(8,128)(2,1)S(1)}, bf16[1024,768]{0,1:T(8,128)(2,1)S(1)}, u32[]{:S(2)}, u32[]{:S(2)}) collective-permute-start(bf16[1024,768]{0,1:T(8,128)(2,1)S(1)} %fusion.87), channel_id=1, source_target_pairs={{0,1},{1,2},{2,3},{3,0},{4,5},{5,6},{6,7},{7,4},{8,9},{9,10},{10,1... | collective-permute-start | bytes 4718600 | tf_op jit(solution)/shard_map/ppermute | solution.py:22
  283.7 48.6 %collective-permute-start.1 = (bf16[1024,768]{0,1:T(8,128)(2,1)S(1)}, bf16[1024,768]{0,1:T(8,128)(2,1)}, u32[]{:S(2)}, u32[]{:S(2)}) collective-permute-start(bf16[1024,768]{0,1:T(8,128)(2,1)S(1)} %collective-permute-done), channel_id=1, source_target_pairs={{0,1},{1,2},{2,3},{3,0},{4,5},{5,6},{6,7},{7,4},{8,9},{9,10},{10,1... | collective-permute-start | bytes 4718600 | tf_op jit(solution)/shard_map/ppermute | solution.py:22
  332.3 21.9 %collective-permute-start.2 = (bf16[1024,768]{0,1:T(8,128)(2,1)}, bf16[1024,768]{0,1:T(8,128)(2,1)}, u32[]{:S(2)}, u32[]{:S(2)}) collective-permute-start(bf16[1024,768]{0,1:T(8,128)(2,1)} %collective-permute-done.1), channel_id=1, source_target_pairs={{0,1},{1,2},{2,3},{3,0},{4,5},{5,6},{6,7},{7,4},{8,9},{9,10},{10,1... | collective-permute-start | bytes 4718600 | tf_op jit(solution)/shard_map/ppermute | solution.py:22
  334.8 197.0 %reduce-scatter.11.cloned.1.call-start = ((), (), s32[]{:S(2)}) async-start(), calls=%async_computation.16 | async-start | bytes 15728640 | tf_op jit(solution)/shard_map/reduce_scatter | solution.py:201
  406.2 19.5 %copy-start.33 = (bf16[768,768]{1,0:T(8,128)(2,1)S(1)}, bf16[768,768]{1,0:T(8,128)(2,1)}, u32[]{:S(2)}) copy-start(bf16[768,768]{1,0:T(8,128)(2,1)} %all-gather.18.cloned.1.call-done) | copy-start | bytes 3538948
  423.1 2.6 copy-start.35
  433.6 1.3 copy-start.34
  433.6 199.9 %reduce-scatter.9.cloned.1.call-start = ((), (), s32[]{:S(2)}) async-start(), calls=%async_computation.15 | async-start | bytes 15728640 | tf_op jit(solution)/shard_map/reduce_scatter | solution.py:175
  447.8 445.2 %reduce-scatter.21.cloned.1.call-start = ((), (), s32[]{:S(2)}) async-start(), calls=%async_computation.21 | async-start | bytes 2654208 | tf_op jit(solution)/shard_map/reduce_scatter | solution.py:228
  459.2 72.6 %copy-start.18 = (f32[1024]{0:T(1024)S(1)}, f32[1024]{0:T(1024)}, u32[]{:S(2)}) copy-start(f32[1024]{0:T(1024)} %copy-done.17) | copy-start | bytes 12292
  459.2 72.6 %copy-start.22 = (f32[768]{0:T(1024)S(1)}, f32[768]{0:T(1024)}, u32[]{:S(2)}) copy-start(f32[768]{0:T(1024)} %copy-done.21) | copy-start | bytes 9220
  459.2 72.6 %copy-start.24 = (f32[1024]{0:T(1024)S(1)}, f32[1024]{0:T(1024)}, u32[]{:S(2)}) copy-start(f32[1024]{0:T(1024)} %copy-done.23) | copy-start | bytes 12292
  459.2 433.8 %reduce-scatter.23.cloned.1.call-start = ((), (), s32[]{:S(2)}) async-start(), calls=%async_computation.22 | async-start | bytes 2654208 | tf_op jit(solution)/shard_map/reduce_scatter | solution.py:229
  459.3 72.5 %copy-start.1 = (f32[1024,768]{0,1:T(8,128)S(1)}, f32[1024,768]{0,1:T(8,128)}, u32[]{:S(2)}) copy-start(f32[1024,768]{0,1:T(8,128)} %copy-done) | copy-start | bytes 9437188
  470.5 163.0 %copy-start.16 = (f32[1024]{0:T(1024)S(1)}, f32[1024]{0:T(1024)}, u32[]{:S(2)}) copy-start(f32[1024]{0:T(1024)} %copy-done.15) | copy-start | bytes 12292
  470.5 422.5 %reduce-scatter.19.cloned.1.call-start = ((), (), s32[]{:S(2)}) async-start(), calls=%async_computation.20 | async-start | bytes 2433024 | tf_op jit(solution)/shard_map/reduce_scatter | solution.py:235
  633.5 6.7 copy-start.13
  640.1 2.6 copy-start.5
  642.7 4.3 copy-start.6
  651.3 336.0 %reduce-scatter.13.cloned.1.call-start = ((), (), s32[]{:S(2)}) async-start(), calls=%async_computation.17 | async-start | bytes 2433024 | tf_op jit(solution)/shard_map/reduce_scatter | solution.py:232
  654.3 160.6 %copy-start.3 = (bf16[1,1024,768]{1,2,0:T(8,128)(2,1)S(1)}, bf16[1,1024,768]{1,2,0:T(8,128)(2,1)}, u32[]{:S(2)}) copy-start(bf16[1,1024,768]{1,2,0:T(8,128)(2,1)} %copy-done.2) | copy-start | bytes 4718596
  654.3 160.6 %copy-start.26 = (f32[1024]{0:T(1024)S(1)}, f32[1024]{0:T(1024)}, u32[]{:S(2)}) copy-start(f32[1024]{0:T(1024)} %copy-done.25) | copy-start | bytes 12292
  654.3 160.6 %copy-start.28 = (f32[768]{0:T(1024)S(1)}, f32[768]{0:T(1024)}, u32[]{:S(2)}) copy-start(f32[768]{0:T(1024)} %copy-done.27) | copy-start | bytes 9220
  654.3 160.6 %copy-start.30 = (f32[1024]{0:T(1024)S(1)}, f32[1024]{0:T(1024)}, u32[]{:S(2)}) copy-start(f32[1024]{0:T(1024)} %copy-done.29) | copy-start | bytes 12292
  814.9 9.4 copy-start.10
  819.8 271.2 %reduce-scatter.15.cloned.1.call-start = ((), (), s32[]{:S(2)}) async-start(), calls=%async_computation.18 | async-start | bytes 2433024 | tf_op jit(solution)/shard_map/reduce_scatter | solution.py:233
  824.3 371.5 %reduce-scatter.17.cloned.1.call-start = ((), (), s32[]{:S(2)}) async-start(), calls=%async_computation.19 | async-start | bytes 2433024 | tf_op jit(solution)/shard_map/reduce_scatter | solution.py:234
  824.3 3.0 copy-start.20
  827.3 1.4 copy-start.8
  830.2 3.6 copy-start.12
  830.2 3.6 copy-start.32
  833.9 1.4 copy-start.11
  833.9 1.7 copy-start.31
Sparse Core Ops, SparseCore 0:
  10.9 56.7 all-gather.11
  70.6 52.9 all-gather.9
  126.5 52.9 all-gather.7
  182.3 52.9 all-gather.13
  237.3 39.9 all-gather.17
  279.3 60.4 all-gather.15
  341.9 41.0 all-gather.19
  433.7 97.9 reduce-scatter.10
  534.4 99.0 reduce-scatter.8
  637.4 68.9 reduce-scatter.20
  710.4 68.1 reduce-scatter.22
  784.3 98.1 reduce-scatter.18
  889.2 98.0 reduce-scatter.12
  993.0 97.9 reduce-scatter.14
  1097.6 98.0 reduce-scatter.16
